TPU v7x, 32 devices: a whole 2x2x4 slice. The times are simulated.
32 devices in a mesh: pts: 2 (over core), cen: 16 (over z, y, x).
Axes of the slice: x: 2, y: 2, z: 4, core: 2. Of those that a mesh axis runs over, the one named last changes fastest.
Arguments:
- points: bfloat16 [2, 1024, 256], P(None, ('pts', 'cen')), may hold values from -4096 to 4096, as said below
- centroids: float32 [16384, 256], P('cen'), may hold values from -6 to 6, as said below
Outputs:
- new_centroids: float32 [16384, 256], P('cen')
- energy: float32 [2, 1024], P(None, 'pts')
Inputs may be any that keep to these rules, and one draw needn't show every extreme that they name: Real-valued points. Real-valued centroids.
All inputs are finite; a program needn't handle non-finite values.
Results may differ from a plain program's by a relative error of at most 0.0003.
The roundings to bfloat16 on the way count: a program that leaves them out, or rounds other values in their place, can miss the bound.
Values may be sent and summed in bfloat16 or wider, within the bound.
A program may use at most 64 MiB of HBM per device.

v0:
```python
import jax
import jax.numpy as jnp
from jax import lax
from jax.sharding import PartitionSpec as P

STEPS = 2
TEMPER = 32.0


def joined(value, axis, join):
    pieces = jax.tree.map(lambda part: lax.all_gather(part, axis), value)
    head = jax.tree.map(lambda part: part[0], pieces)
    tail = jax.tree.map(lambda part: part[1:], pieces)
    running, _ = lax.scan(lambda running, section: (join(running, section), None), head, tail)
    return running


def combine_softmax(first, second):
    top = jnp.maximum(first[0], second[0])
    total = first[1] * jnp.exp(first[0] - top) + second[1] * jnp.exp(second[0] - top)
    return (top, total)


def on_device(points, centroids):
    current = centroids
    energies = []
    for iteration in range(STEPS):
        cent_low = current.astype(jnp.bfloat16)
        cent_sq = jnp.sum(current * current, axis=1)
        segment = lax.all_gather(points[iteration], "cen", axis=0, tiled=True)
        inner = lax.dot_general(
            segment, cent_low, (((1,), (1,)), ((), ())), preferred_element_type=jnp.float32
        )
        logits = (2.0 * inner - cent_sq[None, :]) / TEMPER
        local_top = jnp.max(logits, axis=1)
        local_weights = jnp.exp(logits - local_top[:, None])
        local_total = jnp.sum(local_weights, axis=1)
        top, total = joined((local_top, local_total), "cen", combine_softmax)
        weights = local_weights * jnp.exp(local_top - top)[:, None]
        resp = weights / total[:, None]
        counts = jnp.sum(resp, axis=0)
        sums = lax.dot_general(
            resp.astype(jnp.bfloat16),
            segment,
            (((0,), (0,)), ((), ())),
            preferred_element_type=jnp.float32,
        )
        sums, counts = lax.psum((sums, counts), "pts")
        current = (current + sums) / (1.0 + counts)[:, None]
        energies.append(top + jnp.log(total))
    return (current, jnp.stack(energies))


def solution(mesh):
    placed = (P(None, ("pts", "cen"), None), P("cen", None))
    return jax.shard_map(
        on_device,
        mesh=mesh,
        in_specs=placed,
        out_specs=(P("cen", None), P(None, "pts")),
        check_vma=False,
    )
```

profile of v0, /device:TPU:0, one launch (start us, length us, event | category | flops | bytes accessed | tf_op | source)
XLA Modules:
  0.0 274.8 jit_solution(6816638734251444056)
XLA Ops:
  7.2 0.0 copy-start
  7.2 0.0 all-reduce.3.cloned.1.call-start
  7.2 1.5 multiply_reduce_fusion.1
  8.7 0.7 fusion.14
  9.5 43.8 %all-gather = bf16[1,512,256]{2,1,0:T(8,128)(2,1)S(1)} all-gather(bf16[1,32,256]{2,1,0:T(8,128)(2,1)S(1)} %get-tuple-element.95), channel_id=2, replica_groups=mesh['pts'=2,'cen'=16] {'cen'}, dimensions={1}, use_global_device_ids=true | all-gather | bytes 278528 | tf_op jit(solution)/shard_map/all_gather | solution.py:30
  53.3 0.0 copy-done
  53.3 0.6 fusion.15
  53.8 0.5 fusion
  54.3 35.6 %all-gather.7 = f32[16,1,512]{2,1,0:T(1,128)S(1)} all-gather(f32[1,1,512]{2,1,0:T(1,128)S(1)} %bitcast.65), channel_id=4, replica_groups=mesh['pts'=2,'cen'=16] {'cen'}, dimensions={0}, use_global_device_ids=true | all-gather | bytes 34816 | tf_op jit(solution)/shard_map/all_gather | solution.py:11
  89.9 37.6 %all-gather.6 = f32[16,1,512]{2,1,0:T(1,128)S(1)} all-gather(f32[1,1,512]{2,1,0:T(1,128)S(1)} %bitcast.62), channel_id=3, replica_groups=mesh['pts'=2,'cen'=16] {'cen'}, dimensions={0}, use_global_device_ids=true | all-gather | bytes 34816 | tf_op jit(solution)/shard_map/all_gather | solution.py:11
  127.6 0.8 while.24
  128.4 0.6 fusion.13
  129.0 1.5 fusion.4
  130.4 0.0 all-reduce.3.cloned.1.call-update
  130.4 0.0 all-reduce.5.cloned.1.call-start
  130.5 2.5 psum.29
  133.0 36.8 %all-gather.3 = bf16[1,512,256]{2,1,0:T(8,128)(2,1)S(1)} all-gather(bf16[1,32,256]{2,1,0:T(8,128)(2,1)S(1)} %get-tuple-element.94), channel_id=5, replica_groups=mesh['pts'=2,'cen'=16] {'cen'}, dimensions={1}, use_global_device_ids=true | all-gather | bytes 278528 | tf_op jit(solution)/shard_map/all_gather | solution.py:30
  169.8 1.6 multiply_reduce_fusion
  171.4 0.0 copy-start.1
  171.4 0.5 fusion.16
  171.9 0.4 fusion.1
  172.3 0.1 copy-done.1
  172.4 37.7 %all-gather.9 = f32[16,1,512]{2,1,0:T(1,128)S(1)} all-gather(f32[1,1,512]{2,1,0:T(1,128)S(1)} %bitcast.66), channel_id=7, replica_groups=mesh['pts'=2,'cen'=16] {'cen'}, dimensions={0}, use_global_device_ids=true | all-gather | bytes 34816 | tf_op jit(solution)/shard_map/all_gather | solution.py:11
  210.1 35.6 %all-gather.8 = f32[16,1,512]{2,1,0:T(1,128)S(1)} all-gather(f32[1,1,512]{2,1,0:T(1,128)S(1)} %bitcast.61), channel_id=6, replica_groups=mesh['pts'=2,'cen'=16] {'cen'}, dimensions={0}, use_global_device_ids=true | all-gather | bytes 34816 | tf_op jit(solution)/shard_map/all_gather | solution.py:11
  245.7 0.8 while.25
  246.6 1.6 fusion.2
  248.2 0.0 all-reduce.5.cloned.1.call-update
  248.2 0.5 fusion.8
  248.7 2.5 psum.31
  251.2 0.6 pad_maximum_fusion
  251.8 13.8 %all-reduce.5.cloned.1.call-done = f32[1024,256]{1,0:T(8,128)} async-done(((f32[1024,256]{1,0:T(8,128)}), f32[1024,256]{1,0:T(8,128)}) %all-reduce.5.cloned.1.call-update) | async-done | bytes 1048592 | tf_op jit(solution)/shard_map/psum | solution.py:48
  265.6 2.4 add_divide_fusion
  (79 shorter events, 1.0 us)
Async XLA Ops:
  7.2 46.1 %copy-start = (f32[1024,256]{1,0:T(8,128)S(1)}, f32[1024,256]{1,0:T(8,128)}, u32[]{:S(2)}) copy-start(f32[1024,256]{1,0:T(8,128)} %param.7) | copy-start | bytes 3145732
  7.2 162.7 %all-reduce.3.cloned.1.call-start = ((), (), s32[]{:S(2)}) async-start(), calls=%async_computation | async-start | bytes 2097152 | tf_op jit(solution)/shard_map/psum | solution.py:48
  130.4 135.1 %all-reduce.5.cloned.1.call-start = ((), (), s32[]{:S(2)}) async-start(), calls=%async_computation.1 | async-start | bytes 2097152 | tf_op jit(solution)/shard_map/psum | solution.py:48
  171.4 1.0 copy-start.1
  248.2 17.4 %copy-start.2 = (f32[1024,256]{1,0:T(8,128)S(1)}, f32[1024,256]{1,0:T(8,128)}, u32[]{:S(2)}) copy-start(f32[1024,256]{1,0:T(8,128)} %copy-done.1) | copy-start | bytes 3145732
Sparse Core Ops, SparseCore 0:
  130.6 15.2 all-reduce.2
  248.3 17.1 all-reduce.4
where the time goes:
time: 275 us
  blocking collectives  232 us (84%)
  between operations  14.1 us (5%)
  waiting for transfers between devices  13.8 us (5%)
  other arithmetic  8.64 us (3%)
  matrix products  4.11 us (1%)
    all_gather x4, blocking collectives, joined(): pieces = jax.tree.map(lambda part: lax.all_gather(part, axis), value)  147 us
    all_gather x2, blocking collectives, on_device(): segment = lax.all_gather(points[iteration], 'cen', axis=0, tiled=True)  80.6 us
    psum x2, waiting for transfers between devices, on_device(): sums, counts = lax.psum((sums, counts), 'pts')  13.8 us
  transfers between devices with their start and end apart: 2, of which 1 were waited for; matrix products, arithmetic and copies ran while one was open for 0% of the time, Pallas kernels for 0%

commit v1 on v0

--- a/solution.py
+++ b/solution.py
@@ -5,6 +5,27 @@
 
 STEPS = 2
 TEMPER = 32.0
+
+
+def joined_along(tiles, dim):
+    tiles = jnp.moveaxis(tiles, 0, dim)
+    shape = tiles.shape
+    return tiles.reshape(*shape[:dim], shape[dim] * shape[dim + 1], *shape[dim + 2 :])
+
+
+def collected_by_bits(x, axis):
+    size, position = (lax.axis_size(axis), lax.axis_index(axis))
+    pieces, distance = (x[None], 1)
+    while distance < size:
+        theirs = lax.ppermute(pieces, axis, [(i, i ^ distance) for i in range(size)])
+        low = position & distance == 0
+        pieces = jnp.concatenate([jnp.where(low, pieces, theirs), jnp.where(low, theirs, pieces)])
+        distance *= 2
+    return pieces
+
+
+def gather_by_bits(x, axis, dim):
+    return joined_along(collected_by_bits(x, axis), dim)
 
 
 def joined(value, axis, join):
@@ -27,7 +48,7 @@
     for iteration in range(STEPS):
         cent_low = current.astype(jnp.bfloat16)
         cent_sq = jnp.sum(current * current, axis=1)
-        segment = lax.all_gather(points[iteration], "cen", axis=0, tiled=True)
+        segment = gather_by_bits(points[iteration], "cen", 0)
         inner = lax.dot_general(
             segment, cent_low, (((1,), (1,)), ((), ())), preferred_element_type=jnp.float32
         )

time: 275 us -> 257 us (0.935); the launches traced: 275 us -> 254 us
  blocking collectives: 232 us -> 158 us
  waiting for transfers between devices: 13.8 us -> 36.8 us
  starting transfers between devices: 0.08 us -> 15.2 us
  local copies, waits for them, and re-layouts: 1.24 us -> 13.4 us
    all_gather x2 -> x0, blocking collectives: 80.6 us -> none  [on_device(): segment = lax.all_gather(points[iteration], 'cen', axis=0, tiled=True)]
    ppermute x0 -> x8, starting transfers between devices: none -> 15.1 us  [collected_by_bits(): lax.ppermute(pieces, axis, [(i, i ^ distance) for i in range(size)])]
    ppermute x0 -> x8, waiting for transfers between devices: none -> 14.6 us  [collected_by_bits(): lax.ppermute(pieces, axis, [(i, i ^ distance) for i in range(size)])]
    dynamic_slice x30, local copies, waits for them, and re-layouts: 0.35 us -> 11.4 us  [joined(): lax.scan(lambda running, section: (join(running, section), None), head, t...]
    psum x2, waiting for transfers between devices: 13.8 us -> 22.1 us  [on_device(): sums, counts = lax.psum((sums, counts), 'pts')]
    all_gather x4, blocking collectives: 147 us -> 153 us  [joined(): pieces = jax.tree.map(lambda part: lax.all_gather(part, axis), value)]
  transfers between devices with their start and end apart: 2 -> 10, of which waited for: 1 -> 8; matrix products, arithmetic and copies ran while one was open for 0% -> 7% of each run, Pallas kernels for 0% -> 0%
where the time goes in v1:
time: 257 us; the launch traced here: 254 us
  blocking collectives  158 us (61%)
  waiting for transfers between devices  36.8 us (14%)
  starting transfers between devices  15.2 us (6%)
  between operations  14.2 us (6%)
  local copies, waits for them, and re-layouts  13.4 us (5%)
  other arithmetic  11.3 us (4%)
  matrix products  4.08 us (2%)
    all_gather x4, blocking collectives, joined(): pieces = jax.tree.map(lambda part: lax.all_gather(part, axis), value)  153 us
    psum x2, waiting for transfers between devices, on_device(): sums, counts = lax.psum((sums, counts), 'pts')  22.1 us
    ppermute x8, starting transfers between devices, collected_by_bits(): lax.ppermute(pieces, axis, [(i, i ^ distance) for i in range(size)])  15.1 us
    ppermute x8, waiting for transfers between devices, collected_by_bits(): lax.ppermute(pieces, axis, [(i, i ^ distance) for i in range(size)])  14.6 us
    dynamic_slice x30, local copies, waits for them, and re-layouts, joined(): lax.scan(lambda running, section: (join(running, section), None), head, t...  11.4 us
  transfers between devices with their start and end apart: 10, of which 8 were waited for; matrix products, arithmetic and copies ran while one was open for 7% of the time, Pallas kernels for 0%

profile of v1, /device:TPU:0, one launch (start us, length us, event | category | flops | bytes accessed | tf_op | source)
XLA Modules:
  0.0 253.9 jit_solution(6781056100567142953)
XLA Ops:
  7.2 0.8 slice.35
  8.0 3.0 %collective-permute-start.4 = (bf16[1,32,256]{2,1,0:T(8,128)(2,1)S(1)}, bf16[1,32,256]{2,1,0:T(8,128)(2,1)S(1)}, u32[]{:S(2)}, u32[]{:S(2)}) collective-permute-start(bf16[1,32,256]{2,1,0:T(8,128)(2,1)S(1)} %slice.35), channel_id=1, source_target_pairs={{0,1},{1,0},{2,3},{3,2},{4,5},{5,4},{6,7},{7,6},{8,9},{9,8},{10,11... | collective-permute-start | bytes 49160 | tf_op jit(solution)/shard_map/ppermute | solution.py:20
  11.0 1.7 collective-permute-done.4
  13.4 2.0 collective-permute-start
  15.5 1.7 collective-permute-done
  17.9 2.1 collective-permute-start.1
  20.0 1.4 multiply_reduce_fusion.1
  22.0 2.1 collective-permute-start.2
  24.1 1.5 collective-permute-start.5
  25.6 1.9 collective-permute-done.2
  27.5 2.6 %collective-permute-start.3 = (bf16[8,32,256]{2,1,0:T(8,128)(2,1)S(1)}, bf16[8,32,256]{2,1,0:T(8,128)(2,1)S(1)}, u32[]{:S(2)}, u32[]{:S(2)}) collective-permute-start(bf16[8,32,256]{2,1,0:T(8,128)(2,1)S(1)} %pad_maximum_fusion.2), channel_id=1, source_target_pairs={{0,8},{1,9},{2,10},{3,11},{4,12},{5,13},{6,14},{7,15},{8,0},{9,1},... | collective-permute-start | bytes 393224 | tf_op jit(solution)/shard_map/ppermute | solution.py:20
  30.2 1.6 collective-permute-start.6
  31.9 3.0 %collective-permute-done.3 = bf16[8,32,256]{2,1,0:T(8,128)(2,1)S(1)} collective-permute-done((bf16[8,32,256]{2,1,0:T(8,128)(2,1)S(1)}, bf16[8,32,256]{2,1,0:T(8,128)(2,1)S(1)}, u32[]{:S(2)}, u32[]{:S(2)}) %collective-permute-start.3) | collective-permute-done | bytes 131104 | tf_op jit(solution)/shard_map/ppermute | solution.py:20
  36.0 41.0 %all-gather.5 = f32[16,1,512]{2,1,0:T(1,128)S(1)} all-gather(f32[1,1,512]{2,1,0:T(1,128)S(1)} %bitcast.62), channel_id=3, replica_groups=mesh['pts'=2,'cen'=16] {'cen'}, dimensions={0}, use_global_device_ids=true | all-gather | bytes 34816 | tf_op jit(solution)/shard_map/all_gather | solution.py:32
  77.0 35.8 %all-gather.4 = f32[16,1,512]{2,1,0:T(1,128)S(1)} all-gather(f32[1,1,512]{2,1,0:T(1,128)S(1)} %bitcast.59), channel_id=2, replica_groups=mesh['pts'=2,'cen'=16] {'cen'}, dimensions={0}, use_global_device_ids=true | all-gather | bytes 34816 | tf_op jit(solution)/shard_map/all_gather | solution.py:32
  114.0 11.6 %while.24 = (s32[]{:T(128)}, f32[512]{0:T(512)S(1)}, f32[512]{0:T(512)S(1)}, f32[15,512]{1,0:T(8,128)}, f32[15,512]{1,0:T(8,128)}, /*index=5*/s32[]{:T(128)}) while((s32[]{:T(128)}, f32[512]{0:T(512)S(1)}, f32[512]{0:T(512)S(1)}, f32[15,512]{1,0:T(8,128)}, f32[15,512]{1,0:T(8,128)}, /*index=5*/s32[]{:T(128)}) %tuple.82), condition=%wide.region_4.5_spmd, body=%wide.region_3.4_spmd.sunk | while | flops 3074 | bytes 20553 | solution.py:35
  114.8 0.7 constant_dynamic-slice_fusion.6
  115.6 0.7 constant_dynamic-slice_fusion.6
  116.4 0.7 constant_dynamic-slice_fusion.6
  126.2 1.5 fusion.4
  127.8 0.9 broadcast_select_fusion.5
  128.7 5.9 %collective-permute-done.7 = bf16[8,32,256]{2,1,0:T(8,128)(2,1)S(1)} collective-permute-done((bf16[8,32,256]{2,1,0:T(8,128)(2,1)S(1)}, bf16[8,32,256]{2,1,0:T(8,128)(2,1)S(1)}, u32[]{:S(2)}, u32[]{:S(2)}) %collective-permute-start.7) | collective-permute-done | bytes 131104 | tf_op jit(solution)/shard_map/ppermute | solution.py:20
  134.6 2.5 psum.29
  137.1 7.9 %all-reduce.3.cloned.1.call-done = f32[1024,256]{1,0:T(8,128)} async-done(((f32[1024,256]{1,0:T(8,128)}), f32[1024,256]{1,0:T(8,128)}) %all-reduce.3.cloned.1.call-update) | async-done | bytes 1048592 | tf_op jit(solution)/shard_map/psum | solution.py:69
  145.0 1.6 multiply_reduce_fusion
  147.7 41.0 %all-gather.7 = f32[16,1,512]{2,1,0:T(1,128)S(1)} all-gather(f32[1,1,512]{2,1,0:T(1,128)S(1)} %bitcast.63), channel_id=5, replica_groups=mesh['pts'=2,'cen'=16] {'cen'}, dimensions={0}, use_global_device_ids=true | all-gather | bytes 34816 | tf_op jit(solution)/shard_map/all_gather | solution.py:32
  188.7 35.6 %all-gather.6 = f32[16,1,512]{2,1,0:T(1,128)S(1)} all-gather(f32[1,1,512]{2,1,0:T(1,128)S(1)} %bitcast.58), channel_id=4, replica_groups=mesh['pts'=2,'cen'=16] {'cen'}, dimensions={0}, use_global_device_ids=true | all-gather | bytes 34816 | tf_op jit(solution)/shard_map/all_gather | solution.py:32
  224.3 0.8 while.25
  225.7 1.5 fusion.2
  227.3 2.5 psum.31
  230.3 14.3 %all-reduce.5.cloned.1.call-done = f32[1024,256]{1,0:T(8,128)} async-done(((f32[1024,256]{1,0:T(8,128)}), f32[1024,256]{1,0:T(8,128)}) %all-reduce.5.cloned.1.call-update) | async-done | bytes 1048592 | tf_op jit(solution)/shard_map/psum | solution.py:69
  244.6 2.4 add_divide_fusion
  (109 shorter events, 17.1 us)
Async XLA Ops:
  7.2 27.8 %copy-start = (f32[1024,256]{1,0:T(8,128)S(1)}, f32[1024,256]{1,0:T(8,128)}, u32[]{:S(2)}) copy-start(f32[1024,256]{1,0:T(8,128)} %param.7) | copy-start | bytes 3145732
  7.2 137.8 %all-reduce.3.cloned.1.call-start = ((), (), s32[]{:S(2)}) async-start(), calls=%async_computation | async-start | bytes 2097152 | tf_op jit(solution)/shard_map/psum | solution.py:69
  8.0 4.7 %collective-permute-start.4 = (bf16[1,32,256]{2,1,0:T(8,128)(2,1)S(1)}, bf16[1,32,256]{2,1,0:T(8,128)(2,1)S(1)}, u32[]{:S(2)}, u32[]{:S(2)}) collective-permute-start(bf16[1,32,256]{2,1,0:T(8,128)(2,1)S(1)} %slice.35), channel_id=1, source_target_pairs={{0,1},{1,0},{2,3},{3,2},{4,5},{5,4},{6,7},{7,6},{8,9},{9,8},{10,11... | collective-permute-start | bytes 49160 | tf_op jit(solution)/shard_map/ppermute | solution.py:20
  13.4 3.7 %collective-permute-start = (bf16[1,32,256]{2,1,0:T(8,128)(2,1)S(1)}, bf16[1,32,256]{2,1,0:T(8,128)(2,1)S(1)}, u32[]{:S(2)}, u32[]{:S(2)}) collective-permute-start(bf16[1,32,256]{2,1,0:T(8,128)(2,1)S(1)} %get-tuple-element.112), channel_id=1, source_target_pairs={{0,1},{1,0},{2,3},{3,2},{4,5},{5,4},{6,7},{7,6},{8,9},{9,8},{10,11... | collective-permute-start | bytes 49160 | tf_op jit(solution)/shard_map/ppermute | solution.py:20
  17.9 4.0 %collective-permute-start.1 = (bf16[2,32,256]{2,1,0:T(8,128)(2,1)S(1)}, bf16[2,32,256]{2,1,0:T(8,128)(2,1)S(1)}, u32[]{:S(2)}, u32[]{:S(2)}) collective-permute-start(bf16[2,32,256]{2,1,0:T(8,128)(2,1)S(1)} %pad_maximum_fusion.6), channel_id=1, source_target_pairs={{0,2},{1,3},{2,0},{3,1},{4,6},{5,7},{6,4},{7,5},{8,10},{9,11},{10,... | collective-permute-start | bytes 98312 | tf_op jit(solution)/shard_map/ppermute | solution.py:20
  22.0 5.5 %collective-permute-start.2 = (bf16[4,32,256]{2,1,0:T(8,128)(2,1)S(1)}, bf16[4,32,256]{2,1,0:T(8,128)(2,1)S(1)}, u32[]{:S(2)}, u32[]{:S(2)}) collective-permute-start(bf16[4,32,256]{2,1,0:T(8,128)(2,1)S(1)} %pad_maximum_fusion.4), channel_id=1, source_target_pairs={{0,4},{1,5},{2,6},{3,7},{4,0},{5,1},{6,2},{7,3},{8,12},{9,13},{10,... | collective-permute-start | bytes 196616 | tf_op jit(solution)/shard_map/ppermute | solution.py:20
  24.1 6.1 %collective-permute-start.5 = (bf16[2,32,256]{2,1,0:T(8,128)(2,1)S(1)}, bf16[2,32,256]{2,1,0:T(8,128)(2,1)S(1)}, u32[]{:S(2)}, u32[]{:S(2)}) collective-permute-start(bf16[2,32,256]{2,1,0:T(8,128)(2,1)S(1)} %pad_maximum_fusion.7), channel_id=1, source_target_pairs={{0,2},{1,3},{2,0},{3,1},{4,6},{5,7},{6,4},{7,5},{8,10},{9,11},{10,... | collective-permute-start | bytes 98312 | tf_op jit(solution)/shard_map/ppermute | solution.py:20
  27.5 7.3 %collective-permute-start.3 = (bf16[8,32,256]{2,1,0:T(8,128)(2,1)S(1)}, bf16[8,32,256]{2,1,0:T(8,128)(2,1)S(1)}, u32[]{:S(2)}, u32[]{:S(2)}) collective-permute-start(bf16[8,32,256]{2,1,0:T(8,128)(2,1)S(1)} %pad_maximum_fusion.2), channel_id=1, source_target_pairs={{0,8},{1,9},{2,10},{3,11},{4,12},{5,13},{6,14},{7,15},{8,0},{9,1},... | collective-permute-start | bytes 393224 | tf_op jit(solution)/shard_map/ppermute | solution.py:20
  30.2 97.5 %collective-permute-start.6 = (bf16[4,32,256]{2,1,0:T(8,128)(2,1)S(1)}, bf16[4,32,256]{2,1,0:T(8,128)(2,1)}, u32[]{:S(2)}, u32[]{:S(2)}) collective-permute-start(bf16[4,32,256]{2,1,0:T(8,128)(2,1)S(1)} %pad_maximum_fusion.5), channel_id=1, source_target_pairs={{0,4},{1,5},{2,6},{3,7},{4,0},{5,1},{6,2},{7,3},{8,12},{9,13},{10,... | collective-permute-start | bytes 196616 | tf_op jit(solution)/shard_map/ppermute | solution.py:20
  127.7 116.9 %all-reduce.5.cloned.1.call-start = ((), (), s32[]{:S(2)}) async-start(), calls=%async_computation.1 | async-start | bytes 2097152 | tf_op jit(solution)/shard_map/psum | solution.py:69
  128.7 5.9 %collective-permute-start.7 = (bf16[8,32,256]{2,1,0:T(8,128)(2,1)S(1)}, bf16[8,32,256]{2,1,0:T(8,128)(2,1)S(1)}, u32[]{:S(2)}, u32[]{:S(2)}) collective-permute-start(bf16[8,32,256]{2,1,0:T(8,128)(2,1)S(1)} %pad_maximum_fusion.3), channel_id=1, source_target_pairs={{0,8},{1,9},{2,10},{3,11},{4,12},{5,13},{6,14},{7,15},{8,0},{9,1},... | collective-permute-start | bytes 393224 | tf_op jit(solution)/shard_map/ppermute | solution.py:20
  146.6 1.1 copy-start.1
  225.7 18.9 %copy-start.2 = (f32[1024,256]{1,0:T(8,128)S(1)}, f32[1024,256]{1,0:T(8,128)}, u32[]{:S(2)}) copy-start(f32[1024,256]{1,0:T(8,128)} %copy-done.1) | copy-start | bytes 3145732
Sparse Core Ops, SparseCore 0:
  127.8 17.1 all-reduce.2
  227.4 17.1 all-reduce.4
